TPU v7x, 512 devices: a whole 4x8x8 slice. The times are simulated.
512 devices in a mesh: mem: 8 (over z_hi, core), grid: 64 (over y, x, z_lo).
Axes of the slice: x: 4, y: 8, z: 8 (z_hi: 4, z_lo: 2; z = z_hi * 2 + z_lo), core: 2. Of those that a mesh axis runs over, the one named last changes fastest.
Arguments:
- control: bfloat16 [32, 32, 384, 768], P('mem', None, 'grid'), may hold values from -6 to 6
- perturbation: bfloat16 [32, 32, 768, 384], P('mem', None, 'grid'), may hold values from -6 to 6
- vertical: bfloat16 [32, 32], replicated, may hold values from 0 to 1
- lat_counts: int32 [64], replicated, may hold values from 1 to 6, 361 in all
- lon_counts: int32 [64], replicated, may hold values from 1 to 12, 720 in all
Outputs:
- increment: float32 [32, 768, 384], P('mem', 'grid')
Inputs may be any that keep to these rules, and one draw needn't show every extreme that they name: Slab g holds its first lat_counts[g] latitude slots as real rows, numbered on from the slabs before it. Slab g holds its first lon_counts[g] longitude slots as real columns, numbered on from the slabs before it.
All inputs are finite; a program needn't handle non-finite values.
Results may differ from a plain program's by a relative error of at most 0.0067.
Values may be sent and summed in bfloat16 or wider, within the bound.
A program may use at most 64 MiB of HBM per device.

v0:
```python
import jax
import jax.numpy as jnp
from jax import lax
from jax.sharding import PartitionSpec as P

LAT = 361
LON = 720
LENGTH = 8
BAND = 48


def slot_table(counts, slot_count):
    devices = counts.shape[0]
    slot_ids = jnp.arange(devices * slot_count, dtype=jnp.int32)
    device_of = slot_ids // slot_count
    offset_in = slot_ids - device_of * slot_count
    offsets = jnp.cumsum(counts) - counts
    one_hot = device_of[:, None] == jnp.arange(devices, dtype=jnp.int32)[None, :]
    count_of = jnp.sum(jnp.where(one_hot, counts[None, :], 0), axis=1)
    start_of = jnp.sum(jnp.where(one_hot, offsets[None, :], 0), axis=1)
    return (start_of + offset_in, offset_in < count_of)


def pass_matrix(counts, slot_count, extent, periodic):
    position, usable = slot_table(counts, slot_count)
    lag = position[None, :] - position[:, None]
    if periodic:
        lag = jnp.where(lag < 0, lag + extent, lag)
    steps_f = jnp.arange(0, BAND + 1).astype(jnp.float32)
    normal_sum = jnp.sqrt(jnp.sum(jnp.exp(-2.0 * steps_f / LENGTH)))
    lag_f = lag.astype(jnp.float32)
    inside = (lag >= 0) & (lag <= BAND) & usable[:, None] & usable[None, :]
    weight = jnp.where(inside, jnp.exp(-lag_f / LENGTH) / normal_sum, 0.0)
    return weight.astype(jnp.bfloat16)


def per_device(control, perturbation, vertical, lat_counts, lon_counts):
    groups = lax.axis_size("grid")
    row_slots = control.shape[2]
    lon_pad = control.shape[3]
    col_slots = lon_pad // groups
    lon_matrix = pass_matrix(lon_counts, col_slots, LON, True)
    lat_matrix = pass_matrix(lat_counts, row_slots, LAT, False)
    smooth = jnp.dot(control.reshape(-1, lon_pad), lon_matrix, preferred_element_type=jnp.float32)
    smooth = smooth.astype(jnp.bfloat16).reshape(control.shape)
    columns = lax.all_to_all(smooth, "grid", split_axis=3, concat_axis=2, tiled=True)
    filtered = jnp.einsum(
        "mljc,ji->mlci", columns, lat_matrix, preferred_element_type=jnp.float32
    ).astype(jnp.bfloat16)
    mixed = jnp.einsum("kl,mlci->mkci", vertical, filtered, preferred_element_type=jnp.float32)
    partial_value = jnp.sum(mixed * perturbation.astype(jnp.float32), axis=0)
    summed = lax.psum(partial_value, "mem")
    level_share = partial_value.shape[0] // lax.axis_size("mem")
    return lax.dynamic_slice_in_dim(summed, lax.axis_index("mem") * level_share, level_share, 0)


def solution(mesh):
    in_specs = (P("mem", None, "grid", None), P("mem", None, "grid", None), P(), P(), P())
    out_specs = P("mem", "grid", None)
    return jax.shard_map(
        per_device, mesh=mesh, in_specs=in_specs, out_specs=out_specs, check_vma=False
    )
```

profile of v0, /device:TPU:2, one launch (start us, length us, event | category | flops | bytes accessed | tf_op | source)
XLA Modules:
  0.0 178.7 jit_solution(16469525209210127878)
XLA Ops:
  6.5 0.0 copy-start
  6.5 0.6 exponential_reduce_fusion
  7.2 0.7 copy.27
  7.9 0.1 reduce-window.18
  8.0 0.1 reduce
  8.1 0.7 sub.95
  8.8 0.8 select_reduce_fusion
  10.3 1.9 %copy.28 = bf16[4,32,6,768]{3,2,1,0:T(8,128)(2,1)S(1)} copy(bf16[4,32,6,768]{3,1,2,0:T(8,128)(2,1)} %param.5) | data formatting | bytes 2359296 | tf_op args[0]
  12.2 0.4 reshape.168
  12.7 2.8 %fusion.11 = bf16[768,768]{1,0:T(8,128)(2,1)} fusion(bf16[768,768]{1,0:T(8,128)(2,1)S(1)} %reshape.168, f32[]{:T(128)S(6)} %sqrt.4, s32[768]{0:T(1024)S(1)} %fusion.59, pred[768]{0:T(1024)(128)(4,1)S(1)} %fusion.58), kind=kOutput, calls=%fused_computation.13 | convolution fusion | flops 915406848 | bytes 2363140 | tf_op jit(solution)/shard_map/dot_general | solution.py:44
  15.5 2.2 %reshape.169 = bf16[4,32,6,768]{3,2,1,0:T(8,128)(2,1)S(1)} reshape(bf16[768,768]{1,0:T(8,128)(2,1)} %fusion.11) | data formatting | bytes 2359296 | tf_op jit(solution)/shard_map/reshape | solution.py:45
  17.7 4.6 %copy.29 = bf16[4,32,6,768]{1,0,2,3:T(4,128)(2,1)} copy(bf16[4,32,6,768]{3,2,1,0:T(8,128)(2,1)S(1)} %reshape.169) | data formatting | bytes 2359296 | tf_op jit(solution)/shard_map/reshape | solution.py:45
  22.3 8.1 %reshape.176 = bf16[64,2,4608]{2,1,0:T(2,128)(2,1)} reshape(bf16[768,6,4,32]{3,2,1,0:T(4,128)(2,1)} %bitcast.26) | data formatting | bytes 2359296
  30.4 0.0 copy-start.1
  30.4 12.6 %all-to-all-start = ((bf16[64,2,4608]{2,1,0:T(2,128)(2,1)}), bf16[64,2,4608]{2,1,0:T(2,128)(2,1)S(1)}, u32[]{:S(2)}, u32[]{:S(2)}) async-start(bf16[64,2,4608]{2,1,0:T(2,128)(2,1)} %reshape.176), calls=%async_computation | async-start | bytes 2359296 | tf_op jit(solution)/shard_map/all_to_all | solution.py:46
  43.0 0.0 all-reduce.2.cloned.1.call-start
  43.1 0.0 copy-done.1
  43.1 0.1 copy.32
  43.2 0.1 reduce-window.19
  43.3 0.1 reduce.1
  43.4 0.1 select_reduce_fusion.2
  43.6 30.2 %all-to-all-done = bf16[64,2,4608]{2,1,0:T(2,128)(2,1)S(1)} async-done(((bf16[64,2,4608]{2,1,0:T(2,128)(2,1)}), bf16[64,2,4608]{2,1,0:T(2,128)(2,1)S(1)}, u32[]{:S(2)}, u32[]{:S(2)}) %all-to-all-start) | async-done | bytes 1179680 | tf_op jit(solution)/shard_map/all_to_all | solution.py:46
  73.8 4.1 %reshape.177 = bf16[768,6,4,32]{3,2,1,0:T(4,128)(2,1)} reshape(bf16[64,2,4608]{2,1,0:T(2,128)(2,1)S(1)} %all-to-all-done) | data formatting | bytes 2359296
  77.8 0.0 copy-start.2
  77.8 6.2 %copy.31 = bf16[4,32,64,6,12]{1,0,4,3,2:T(4,128)(2,1)} copy(bf16[4,32,64,6,12]{1,0,3,4,2:T(4,128)(2,1)} %bitcast.27) | data formatting | bytes 2359296 | tf_op jit(solution)/shard_map/all_to_all | solution.py:46
  84.0 0.0 copy-done
  84.0 0.0 copy-done.2
  84.0 5.9 %fusion.2 = f32[32,12,384]{2,0,1:T(8,128)} fusion(bf16[4,32,12,384]{3,1,2,0:T(8,128)(2,1)S(1)} %copy-done.2, bf16[4,32,384,12]{1,0,3,2:T(4,128)(2,1)} %bitcast.28, f32[]{:T(128)S(6)} %sqrt.4, s32[384]{0:T(512)S(1)} %fusion.64, pred[384]{0:T(512)(128)(4,1)S(1)} %fusion.63, bf16[32,32]{1,0:T(8,128)(2,1)S(1)} %copy-done), kind=kOutput, calls=%fused_computation.4 | convolution fusion | flops 494714880 | bytes 2953092 | tf_op jit(solution)/shard_map/kl,mlci->mkci/dot_general | solution.py:50
  89.9 0.0 all-reduce.2.cloned.1.call-update
  90.0 80.3 %all-reduce.2.cloned.1.call-done = f32[32,12,384]{2,0,1:T(8,128)} async-done(((f32[32,12,384]{2,0,1:T(8,128)}), f32[32,12,384]{2,0,1:T(8,128)}) %all-reduce.2.cloned.1.call-update) | async-done | bytes 589840 | tf_op jit(solution)/shard_map/psum | solution.py:52
  170.3 1.6 constant_dynamic-slice_fusion
  (7 shorter events, 0.1 us)
Async XLA Ops:
  6.5 77.5 %copy-start = (bf16[32,32]{1,0:T(8,128)(2,1)S(1)}, bf16[32,32]{1,0:T(8,128)(2,1)}, u32[]{:S(2)}) copy-start(bf16[32,32]{1,0:T(8,128)(2,1)} %param.7) | copy-start | bytes 6148
  30.4 12.7 %copy-start.1 = (s32[64]{0:T(128)S(1)}, s32[64]{0:T(128)}, u32[]{:S(2)}) copy-start(s32[64]{0:T(128)} %param.8) | copy-start | bytes 772
  30.4 43.3 %all-to-all-start = ((bf16[64,2,4608]{2,1,0:T(2,128)(2,1)}), bf16[64,2,4608]{2,1,0:T(2,128)(2,1)S(1)}, u32[]{:S(2)}, u32[]{:S(2)}) async-start(bf16[64,2,4608]{2,1,0:T(2,128)(2,1)} %reshape.176), calls=%async_computation | async-start | bytes 2359296 | tf_op jit(solution)/shard_map/all_to_all | solution.py:46
  43.0 127.2 %all-reduce.2.cloned.1.call-start = ((), (), s32[]{:S(2)}) async-start(), calls=%async_computation.1 | async-start | bytes 1179648 | tf_op jit(solution)/shard_map/psum | solution.py:52
  77.8 6.2 %copy-start.2 = (bf16[4,32,12,384]{3,1,2,0:T(8,128)(2,1)S(1)}, bf16[4,32,12,384]{3,1,2,0:T(8,128)(2,1)}, u32[]{:S(2)}) copy-start(bf16[4,32,12,384]{3,1,2,0:T(8,128)(2,1)} %param.6) | copy-start | bytes 3538948
Sparse Core Ops, SparseCore 0:
  90.1 80.1 all-reduce.1
where the time goes:
time: 179 us
  waiting for transfers between devices  111 us (62%)
  local copies, waits for them, and re-layouts  30 us (17%)
  between operations  14.2 us (8%)
  starting transfers between devices  12.6 us (7%)
  matrix products  8.74 us (5%)
  other arithmetic  2.63 us (1%)
    psum x1, waiting for transfers between devices, per_device(): summed = lax.psum(partial_value, 'mem')  80.3 us
    all_to_all x1, waiting for transfers between devices, per_device(): lax.all_to_all(smooth, 'grid', split_axis=3, concat_axis=2, tiled=True)  30.2 us
    unnamed x9, local copies, waits for them, and re-layouts  14.2 us
    all_to_all x1, starting transfers between devices, per_device(): lax.all_to_all(smooth, 'grid', split_axis=3, concat_axis=2, tiled=True)  12.6 us
    reshape x2, local copies, waits for them, and re-layouts, per_device(): smooth = smooth.astype(jnp.bfloat16).reshape(control.shape)  6.78 us
    all_to_all x1, local copies, waits for them, and re-layouts, per_device(): lax.all_to_all(smooth, 'grid', split_axis=3, concat_axis=2, tiled=True)  6.17 us
    dot_general x1, matrix products, per_device(): jnp.einsum('kl,mlci->mkci', vertical, filtered, preferred_element_type=jn...  5.9 us
  transfers between devices with their start and end apart: 2, of which 2 were waited for; matrix products, arithmetic and copies ran while one was open for 0% of the time, Pallas kernels for 0%

commit v1 on v0

--- a/solution.py
+++ b/solution.py
@@ -43,7 +43,15 @@
     lat_matrix = pass_matrix(lat_counts, row_slots, LAT, False)
     smooth = jnp.dot(control.reshape(-1, lon_pad), lon_matrix, preferred_element_type=jnp.float32)
     smooth = smooth.astype(jnp.bfloat16).reshape(control.shape)
-    columns = lax.all_to_all(smooth, "grid", split_axis=3, concat_axis=2, tiled=True)
+    columns = jnp.concatenate(
+        lax.all_to_all(
+            jnp.stack(jnp.split(smooth, lax.axis_size("grid"), 3)),
+            axis_name="grid",
+            split_axis=0,
+            concat_axis=0,
+        ),
+        2,
+    )
     filtered = jnp.einsum(
         "mljc,ji->mlci", columns, lat_matrix, preferred_element_type=jnp.float32
     ).astype(jnp.bfloat16)

time: 179 us -> 244 us (1.36)
  local copies, waits for them, and re-layouts: 30 us -> 94.4 us
    unnamed x9 -> x72, local copies, waits for them, and re-layouts: 14.2 us -> 67.2 us
    another operation x2 -> x4, local copies, waits for them, and re-layouts: 0.84 us -> 22.8 us  [the longest x2 22 us: per_device(): jnp.stack(jnp.split(smooth, lax.axis_size('grid'), 3))]
    all_to_all x1 -> x0, local copies, waits for them, and re-layouts: 6.17 us -> none  [per_device(): lax.all_to_all(smooth, 'grid', split_axis=3, concat_axis=2, tiled=True)]
    reshape x2 -> x1, local copies, waits for them, and re-layouts: 6.78 us -> 2.41 us  [per_device(): smooth = smooth.astype(jnp.bfloat16).reshape(control.shape)]
where the time goes in v1:
time: 244 us; the launch traced here: 243 us
  waiting for transfers between devices  111 us (45%)
  local copies, waits for them, and re-layouts  94.4 us (39%)
  between operations  14.2 us (6%)
  starting transfers between devices  12.5 us (5%)
  matrix products  8.71 us (4%)
  other arithmetic  2.63 us (1%)
    psum x1, waiting for transfers between devices, per_device(): summed = lax.psum(partial_value, 'mem')  80.4 us
    unnamed x72, local copies, waits for them, and re-layouts  67.2 us
    all_to_all x1, waiting for transfers between devices, per_device(): lax.all_to_all(jnp.stack(jnp.split(smooth, lax.axis_size('grid'), 3)), ax...  30.2 us
    another operation x2, local copies, waits for them, and re-layouts, per_device(): jnp.stack(jnp.split(smooth, lax.axis_size('grid'), 3))  22 us
    all_to_all x1, starting transfers between devices, per_device(): lax.all_to_all(jnp.stack(jnp.split(smooth, lax.axis_size('grid'), 3)), ax...  12.5 us
    dot_general x1, matrix products, per_device(): jnp.einsum('kl,mlci->mkci', vertical, filtered, preferred_element_type=jn...  5.87 us
  transfers between devices with their start and end apart: 2, of which 2 were waited for; matrix products, arithmetic and copies ran while one was open for 0% of the time, Pallas kernels for 0%

profile of v1, /device:TPU:2, one launch (start us, length us, event | category | flops | bytes accessed | tf_op | source)
XLA Modules:
  0.0 243.1 jit_solution(762742676908442568)
XLA Ops:
  10.3 1.9 copy.82
  12.7 2.8 %fusion.11 = bf16[768,768]{1,0:T(8,128)(2,1)} fusion(bf16[768,768]{1,0:T(8,128)(2,1)S(1)} %reshape.174, f32[]{:T(128)S(6)} %sqrt.4, s32[768]{0:T(1024)S(1)} %fusion.123, pred[768]{0:T(1024)(128)(4,1)S(1)} %fusion.122), kind=kOutput, calls=%fused_computation.13 | convolution fusion | flops 915406848 | bytes 2363140 | tf_op jit(solution)/shard_map/dot_general | solution.py:44
  15.5 2.4 reshape.175
  18.7 0.8 fusion.116
  19.5 0.8 fusion.115
  20.3 0.9 fusion.114
  21.2 0.9 fusion.113
  22.1 0.9 fusion.112
  22.9 0.8 fusion.111
  23.8 0.8 fusion.110
  24.6 0.9 fusion.109
  25.5 0.8 fusion.108
  26.3 0.8 fusion.107
  27.1 0.9 fusion.106
  28.0 0.9 fusion.105
  28.9 0.8 fusion.104
  30.6 0.8 fusion.102
  32.2 0.8 fusion.100
  33.1 0.8 fusion.99
  33.9 0.9 fusion.98
  34.8 0.8 fusion.97
  35.6 0.9 fusion.96
  36.5 0.8 fusion.95
  37.3 0.8 fusion.94
  38.2 0.8 fusion.93
  39.0 0.8 fusion.92
  39.9 0.9 fusion.91
  40.7 0.9 fusion.90
  41.6 0.8 fusion.89
  44.1 0.9 fusion.86
  45.7 0.8 fusion.84
  46.5 0.9 fusion.83
  47.4 0.9 fusion.82
  48.3 0.8 fusion.81
  49.1 0.9 fusion.80
  50.0 0.9 fusion.79
  50.8 0.9 fusion.78
  51.7 0.9 fusion.77
  52.5 0.9 fusion.76
  53.4 0.9 fusion.75
  55.1 0.8 fusion.73
  56.7 0.8 fusion.71
  57.6 0.9 fusion.70
  58.4 0.8 fusion.69
  59.3 0.8 fusion.68
  60.1 0.9 fusion.67
  61.0 0.8 fusion.66
  64.3 0.8 fusion.62
  65.2 0.8 fusion.61
  66.0 0.9 fusion.60
  66.9 0.9 fusion.59
  67.7 0.8 fusion.58
  68.6 0.8 fusion.57
  69.4 0.8 fusion.56
  70.3 0.8 fusion.55
  71.1 0.8 fusion.54
  72.0 21.1 %copy.83 = bf16[64,4,32,6,12]{2,1,4,3,0:T(4,128)(2,1)} copy(bf16[64,4,32,6,12]{4,3,2,1,0:T(8,128)(2,1)} %fusion.54) | data formatting | bytes 2359296 | tf_op jit(solution)/shard_map/stack | solution.py:48
  93.1 8.1 %reshape.184 = bf16[64,2,4608]{2,1,0:T(2,128)(2,1)} reshape(bf16[64,6,12,4,32]{4,3,2,1,0:T(4,128)(2,1)} %bitcast.281) | data formatting | bytes 2359296
  101.2 12.5 %all-to-all-start = ((bf16[64,2,4608]{2,1,0:T(2,128)(2,1)}), bf16[64,2,4608]{2,1,0:T(2,128)(2,1)S(1)}, u32[]{:S(2)}, u32[]{:S(2)}) async-start(bf16[64,2,4608]{2,1,0:T(2,128)(2,1)} %reshape.184), calls=%async_computation | async-start | bytes 2359296 | tf_op jit(solution)/shard_map/all_to_all | solution.py:47
  114.2 30.2 %all-to-all-done = bf16[64,2,4608]{2,1,0:T(2,128)(2,1)S(1)} async-done(((bf16[64,2,4608]{2,1,0:T(2,128)(2,1)}), bf16[64,2,4608]{2,1,0:T(2,128)(2,1)S(1)}, u32[]{:S(2)}, u32[]{:S(2)}) %all-to-all-start) | async-done | bytes 1179680 | tf_op jit(solution)/shard_map/all_to_all | solution.py:47
  144.4 4.0 %reshape.185 = bf16[64,6,12,4,32]{4,3,2,1,0:T(4,128)(2,1)} reshape(bf16[64,2,4608]{2,1,0:T(2,128)(2,1)S(1)} %all-to-all-done) | data formatting | bytes 2359296
  148.4 5.9 %fusion.2 = f32[32,12,384]{2,0,1:T(8,128)} fusion(bf16[4,32,12,384]{3,1,2,0:T(8,128)(2,1)S(1)} %copy-done.2, bf16[4,32,384,12]{1,0,3,2:T(4,128)(2,1)} %bitcast.282, f32[]{:T(128)S(6)} %sqrt.4, s32[384]{0:T(512)S(1)} %fusion.128, pred[384]{0:T(512)(128)(4,1)S(1)} %fusion.127, bf16[32,32]{1,0:T(8,128)(2,1)S(1)} %copy-done), kind=kOutput, calls=%fused_computation.4 | convolution fusion | flops 494714880 | bytes 2953092 | tf_op jit(solution)/shard_map/kl,mlci->mkci/dot_general | solution.py:58
  154.3 80.4 %all-reduce.2.cloned.1.call-done = f32[32,12,384]{2,0,1:T(8,128)} async-done(((f32[32,12,384]{2,0,1:T(8,128)}), f32[32,12,384]{2,0,1:T(8,128)}) %all-reduce.2.cloned.1.call-update) | async-done | bytes 589840 | tf_op jit(solution)/shard_map/psum | solution.py:60
  234.7 1.6 constant_dynamic-slice_fusion
  (37 shorter events, 12.9 us)
Async XLA Ops:
  6.5 141.9 %copy-start = (bf16[32,32]{1,0:T(8,128)(2,1)S(1)}, bf16[32,32]{1,0:T(8,128)(2,1)}, u32[]{:S(2)}) copy-start(bf16[32,32]{1,0:T(8,128)(2,1)} %param.7) | copy-start | bytes 6148
  66.0 47.7 %copy-start.1 = (s32[64]{0:T(128)S(1)}, s32[64]{0:T(128)}, u32[]{:S(2)}) copy-start(s32[64]{0:T(128)} %param.8) | copy-start | bytes 772
  72.0 76.4 %copy-start.2 = (bf16[4,32,12,384]{3,1,2,0:T(8,128)(2,1)S(1)}, bf16[4,32,12,384]{3,1,2,0:T(8,128)(2,1)}, u32[]{:S(2)}) copy-start(bf16[4,32,12,384]{3,1,2,0:T(8,128)(2,1)} %param.6) | copy-start | bytes 3538948
  101.2 43.2 %all-to-all-start = ((bf16[64,2,4608]{2,1,0:T(2,128)(2,1)}), bf16[64,2,4608]{2,1,0:T(2,128)(2,1)S(1)}, u32[]{:S(2)}, u32[]{:S(2)}) async-start(bf16[64,2,4608]{2,1,0:T(2,128)(2,1)} %reshape.184), calls=%async_computation | async-start | bytes 2359296 | tf_op jit(solution)/shard_map/all_to_all | solution.py:47
  113.7 121.0 %all-reduce.2.cloned.1.call-start = ((), (), s32[]{:S(2)}) async-start(), calls=%async_computation.1 | async-start | bytes 1179648 | tf_op jit(solution)/shard_map/psum | solution.py:60
Sparse Core Ops, SparseCore 0:
  154.4 80.2 all-reduce.1
